TPU v7x, 32 devices: a whole 2x2x4 slice. The times are simulated.
32 devices in a mesh: table: 16 (over z, y, x), narrow: 2 (over core).
Axes of the slice: x: 2, y: 2, z: 4, core: 2. Of those that a mesh axis runs over, the one named last changes fastest.
Arguments:
- table_rows: bfloat16 [16384, 256], P('table'), may hold values from -3 to 3
- accum: float32 [16384], P('table'), may hold values from 1 to 100
- factor_down: bfloat16 [2048, 256], P('narrow'), may hold values from -0.125 to 0.125
- factor_up: bfloat16 [2048, 256], P('narrow'), may hold values from -0.375 to 0.375
- cross_bias: float32 [2048], replicated, may hold values from -3 to 3
- out_weight: bfloat16 [2048], replicated, may hold values from -0.125 to 0.125
- target: float32 [4096], P(('table', 'narrow')), may hold values from 0 to 1
- bag_rows: int32 [512, 512], P(('table', 'narrow')), may hold values from -1 to 1023, as said below
- slot_target: int32 [512, 128], P(('table', 'narrow')), may hold values from -1 to 1023, as said below
Outputs:
- logits: float32 [4096], P(('table', 'narrow'))
- down_grad: float32 [2048, 256], P('narrow')
- up_grad: float32 [2048, 256], P('narrow')
- new_rows: bfloat16 [16384, 256], P('table')
- new_accum: float32 [16384], P(('table', 'narrow'))
Inputs may be any that keep to these rules, and one draw needn't show every extreme that they name: `slot_target`: for each source device (its 16 rows): every bag 0 .. 1023 is named by exactly one slot and the other slots hold -1; in every draw each source device has one window all of whose 128 slots are used. `bag_rows`: A used slot holds 1 to 4 rows of the window first and -1 after them; an unused slot holds -1 only; each source device has a slot with 4 lookups.
All inputs are finite; a program needn't handle non-finite values.
Results may differ from a plain program's by a relative error of at most 0.0077.
Values may be sent and summed in bfloat16 or wider, within the bound.
No kernel may reach another device: no remote copies, remote signals or barrier semaphores. Data moves between devices by JAX's collectives and lax.ppermute only.
A program may use at most 64 MiB of HBM per device.

v0:
```python
import math
import jax
import jax.numpy as jnp
from jax import lax
from jax.sharding import PartitionSpec as P

FEAT = 8
HOT = 4
LEARN_RATE = 0.2
LOSS_SCALE = 32.0
ADA_EPS = 1e-06


def transposed_dot(left, right):
    return lax.dot_general(
        left, right, (((0,), (0,)), ((), ())), preferred_element_type=jnp.float32
    )


def rows_dot(left, right):
    return lax.dot_general(
        left, right, (((1,), (1,)), ((), ())), preferred_element_type=jnp.float32
    )


def local(
    table_rows, accum, factor_down, factor_up, cross_bias, out_weight, target, bag_rows, slot_target
):
    tables = lax.axis_size("table")
    narrows = lax.axis_size("narrow")
    row_dev, emb_width = table_rows.shape
    pools_per = slot_target.shape[1]
    samples = target.shape[0]
    bag_count = samples * FEAT
    slot_count = tables * pools_per
    asked = lax.all_to_all(bag_rows, "table", split_axis=0, concat_axis=0, tiled=True)
    lookup_ids = asked.reshape(slot_count, HOT)
    positions = lax.broadcasted_iota(jnp.int32, (1, row_dev), 1)
    counts = jnp.zeros((slot_count, row_dev), jnp.bfloat16)
    for lookup in range(HOT):
        counts = counts + (lookup_ids[:, lookup : lookup + 1] == positions).astype(jnp.bfloat16)
    pool_sums = jnp.dot(counts, table_rows, preferred_element_type=jnp.float32)
    pool_out = pool_sums.astype(jnp.bfloat16).reshape(tables, pools_per, emb_width)
    arrived = lax.all_to_all(pool_out, "table", split_axis=0, concat_axis=0, tiled=True).reshape(
        slot_count, emb_width
    )
    bag_index = lax.broadcasted_iota(jnp.int32, (bag_count, 1), 0)
    placing = (slot_target.reshape(1, slot_count) == bag_index).astype(jnp.bfloat16)
    pooled_feats = (
        jnp.dot(placing, arrived, preferred_element_type=jnp.float32)
        .astype(jnp.bfloat16)
        .reshape(samples, FEAT * emb_width)
    )
    down_full, up_full = (
        lax.all_gather(factor_down, "narrow", axis=0, tiled=True),
        lax.all_gather(factor_up, "narrow", axis=0, tiled=True),
    )
    hidden = jnp.dot(pooled_feats, down_full, preferred_element_type=jnp.float32).astype(
        jnp.bfloat16
    )
    cross_out = rows_dot(hidden, up_full)
    feats_f = pooled_feats.astype(jnp.float32)
    shifted = cross_out + cross_bias
    mixed_out = feats_f * shifted + feats_f
    weight_f = out_weight.astype(jnp.float32)
    logits = jnp.sum(mixed_out * weight_f, axis=1)
    dlogit = LOSS_SCALE * (jax.nn.sigmoid(logits) - target)
    dmixed = dlogit[:, None] * weight_f
    dcross = (dmixed * feats_f).astype(jnp.bfloat16)
    dhidden = jnp.dot(dcross, up_full, preferred_element_type=jnp.float32).astype(jnp.bfloat16)
    back_term = rows_dot(dhidden, down_full)
    dpooled = (dmixed * (shifted + 1.0) + back_term).astype(jnp.bfloat16)
    narrow_sum = lax.psum_scatter(
        jnp.concatenate(
            [transposed_dot(pooled_feats, dhidden), transposed_dot(dcross, hidden)], axis=1
        ).astype(jnp.bfloat16),
        "narrow",
        scatter_dimension=0,
        tiled=True,
    ).astype(jnp.float32)
    grand_total = lax.psum(narrow_sum, "table")
    batch_all = samples * tables * narrows
    grand_total = grand_total * (1.0 / math.sqrt(batch_all))
    rank_size = factor_down.shape[1]
    down_grad = grand_total[:, :rank_size]
    up_grad = grand_total[:, rank_size:]
    bag_grads = dpooled.reshape(bag_count, emb_width)
    slot_grads = (
        transposed_dot(placing, bag_grads)
        .astype(jnp.bfloat16)
        .reshape(tables, pools_per, emb_width)
    )
    returned = lax.all_to_all(slot_grads, "table", split_axis=0, concat_axis=0, tiled=True).reshape(
        slot_count, emb_width
    )
    local_grad = transposed_dot(counts, returned)
    narrow_index = lax.axis_index("narrow")
    share_size = row_dev // narrows
    row_grad = lax.psum(local_grad.astype(jnp.bfloat16), "narrow").astype(jnp.float32)
    accum_all = accum + jnp.mean(row_grad * row_grad, axis=1)
    new_rows = (
        table_rows.astype(jnp.float32)
        - LEARN_RATE * row_grad * lax.rsqrt(accum_all + ADA_EPS)[:, None]
    ).astype(jnp.bfloat16)
    new_accum = lax.dynamic_slice_in_dim(accum_all, narrow_index * share_size, share_size, 0)
    return (logits, down_grad, up_grad, new_rows, new_accum)


def solution(mesh):
    in_specs = (
        P("table", None),
        P("table"),
        P("narrow", None),
        P("narrow", None),
        P(),
        P(),
        P(("table", "narrow")),
        P(("table", "narrow"), None),
        P(("table", "narrow"), None),
    )
    out_specs = (
        P(("table", "narrow")),
        P("narrow", None),
        P("narrow", None),
        P("table", None),
        P(("table", "narrow")),
    )
    return jax.shard_map(local, mesh=mesh, in_specs=in_specs, out_specs=out_specs, check_vma=False)
```

profile of v0, /device:TPU:0, one launch (start us, length us, event | category | flops | bytes accessed | tf_op | source)
XLA Modules:
  0.0 247.3 jit_solution(3443778541291321474)
XLA Ops:
  7.2 0.8 all_to_all.12
  8.0 15.5 %all_to_all.19 = s32[16,1,512]{2,1,0:T(1,128)S(1)} all-to-all(s32[16,1,512]{2,1,0:T(1,128)S(1)} %all_to_all.12), channel_id=1, replica_groups=mesh['table'=16,'narrow'=2] {'table'}, dimensions={0} | all-to-all | bytes 65536 | tf_op jit(solution)/shard_map/all_to_all | solution.py:36
  23.5 1.1 reshape.40
  24.6 2.0 slice_reduce_fusion.3
  26.6 6.1 %fusion.15 = bf16[2048,256]{1,0:T(8,128)(2,1)} fusion(bf16[1024,256]{1,0:T(8,128)(2,1)S(1)} %copy-done.2, s32[2048]{0:T(1024)S(1)} %get-tuple-element.21, s32[2048]{0:T(1024)S(1)} %get-tuple-element.22, s32[2048]{0:T(1024)S(1)} %get-tuple-element.23, s32[2048]{0:T(1024)S(1)} %get-tuple-element.20), kind=kOutput, calls=%fused_computation.18 | convolution fusion | flops 1107820544 | bytes 1605632 | tf_op jit(solution)/shard_map/dot_general | solution.py:42
  32.7 3.8 %all-to-all-start.1 = ((bf16[16,128,256]{2,1,0:T(8,128)(2,1)}), bf16[16,128,256]{2,1,0:T(8,128)(2,1)S(1)}, u32[]{:S(2)}, u32[]{:S(2)}) async-start(bf16[16,128,256]{2,1,0:T(8,128)(2,1)} %bitcast.1), calls=%async_computation.1 | async-start | bytes 2097152 | tf_op jit(solution)/shard_map/all_to_all | solution.py:44
  36.5 0.7 all-gather.3.cloned.1.call-update
  37.3 0.7 all-gather.5.cloned.1.call-update
  38.0 21.7 %all-to-all-done.1 = bf16[16,128,256]{2,1,0:T(8,128)(2,1)S(1)} async-done(((bf16[16,128,256]{2,1,0:T(8,128)(2,1)}), bf16[16,128,256]{2,1,0:T(8,128)(2,1)S(1)}, u32[]{:S(2)}, u32[]{:S(2)}) %all-to-all-start.1) | async-done | bytes 1048608 | tf_op jit(solution)/shard_map/all_to_all | solution.py:44
  59.8 1.5 fusion.23
  61.2 0.2 reshape.43
  61.5 1.5 convolution_convert_fusion.3
  63.1 2.0 fusion.29
  65.1 0.4 convolution_convert_fusion.2
  65.5 0.5 fusion.19
  66.0 0.2 reshape.44
  66.3 3.3 %fusion.18 = bf16[2048,256]{1,0:T(8,128)(2,1)} fusion(bf16[1024,256]{1,0:T(8,128)(2,1)S(1)} %reshape.44, s32[2048]{0:T(1024)S(1)} %bitcast.22), kind=kOutput, calls=%fused_computation.19 | convolution fusion | flops 1076363264 | bytes 1581056 | tf_op jit(solution)/shard_map/dot_general | solution.py:15
  69.6 5.8 %all-to-all-start.2 = ((bf16[16,128,256]{2,1,0:T(8,128)(2,1)}), bf16[16,128,256]{2,1,0:T(8,128)(2,1)S(1)}, u32[]{:S(2)}, u32[]{:S(2)}) async-start(bf16[16,128,256]{2,1,0:T(8,128)(2,1)} %bitcast.3), calls=%async_computation.3 | async-start | bytes 2097152 | tf_op jit(solution)/shard_map/all_to_all | solution.py:93
  75.6 0.5 convolution_convert_fusion
  76.2 23.0 %all-to-all-done.2 = bf16[16,128,256]{2,1,0:T(8,128)(2,1)S(1)} async-done(((bf16[16,128,256]{2,1,0:T(8,128)(2,1)}), bf16[16,128,256]{2,1,0:T(8,128)(2,1)S(1)}, u32[]{:S(2)}, u32[]{:S(2)}) %all-to-all-start.2) | async-done | bytes 1048608 | tf_op jit(solution)/shard_map/all_to_all | solution.py:93
  99.1 5.5 %fusion.20 = bf16[1024,256]{1,0:T(8,128)(2,1)} fusion(bf16[2048,256]{1,0:T(8,128)(2,1)S(1)} %bitcast.20, s32[2048]{0:T(1024)S(1)} %get-tuple-element.21, s32[2048]{0:T(1024)S(1)} %get-tuple-element.22, s32[2048]{0:T(1024)S(1)} %get-tuple-element.23, s32[2048]{0:T(1024)S(1)} %get-tuple-element.20), kind=kOutput, calls=%fused_computation.31 | convolution fusion | flops 1107558400 | bytes 1605632 | tf_op jit(solution)/shard_map/dot_general | solution.py:15
  104.7 0.5 convolution_convert_fusion.1
  105.2 1.5 pad_maximum_fusion
  106.7 17.0 %all-reduce.3.cloned.1.call-done = bf16[1024,256]{1,0:T(8,128)(2,1)} async-done(((bf16[1024,256]{1,0:T(8,128)(2,1)}), bf16[1024,256]{1,0:T(8,128)(2,1)}) %all-reduce.3.cloned.1.call-update) | async-done | bytes 524304 | tf_op jit(solution)/shard_map/psum | solution.py:99
  123.7 1.3 fusion.24
  125.0 0.7 dynamic_slice.3
  125.7 2.1 fusion.26
  127.8 8.9 %reduce-scatter.2.cloned.1.call-done = bf16[1024,512]{0,1:T(8,128)(2,1)} async-done(((bf16[2048,512]{0,1:T(8,128)(2,1)}), bf16[1024,512]{0,1:T(8,128)(2,1)}) %reduce-scatter.2.cloned.1.call-update) | async-done | bytes 1048592 | tf_op jit(solution)/shard_map/reduce_scatter | solution.py:73
  136.7 100.9 %all-reduce.4 = f32[1024,512]{0,1:T(8,128)S(1)} all-reduce(bf16[1024,512]{0,1:T(8,128)(2,1)} %reduce-scatter.2.cloned.1.call-done), channel_id=1, replica_groups=mesh['table'=16,'narrow'=2] {'table'}, use_global_device_ids=true, to_apply=%region_2.0 | all-reduce | flops 524288 | bytes 3145728 | tf_op jit(solution)/shard_map/psum | solution.py:81
  237.9 0.2 fusion.33
  238.2 1.3 copy.19
  239.5 1.3 copy.18
  (31 shorter events, 0.8 us)
Async XLA Ops:
  24.6 2.0 copy-start.2
  32.7 5.3 %copy-start.4 = (bf16[2048]{0:T(1024)(128)(2,1)S(1)}, bf16[2048]{0:T(1024)(128)(2,1)}, u32[]{:S(2)}) copy-start(bf16[2048]{0:T(1024)(128)(2,1)} %param.14) | copy-start | bytes 12292
  32.7 27.1 %copy-start.7 = (s32[16,128]{1,0:T(8,128)S(1)}, s32[16,128]{1,0:T(8,128)}, u32[]{:S(2)}) copy-start(s32[16,128]{1,0:T(8,128)} %param.17) | copy-start | bytes 24580
  32.7 27.1 %all-to-all-start.1 = ((bf16[16,128,256]{2,1,0:T(8,128)(2,1)}), bf16[16,128,256]{2,1,0:T(8,128)(2,1)S(1)}, u32[]{:S(2)}, u32[]{:S(2)}) async-start(bf16[16,128,256]{2,1,0:T(8,128)(2,1)} %bitcast.1), calls=%async_computation.1 | async-start | bytes 2097152 | tf_op jit(solution)/shard_map/all_to_all | solution.py:44
  36.5 25.0 %all-gather.3.cloned.1.call-start = ((), (), s32[]{:S(2)}) async-start(), calls=%async_computation.4 | async-start | bytes 1572864 | tf_op jit(solution)/shard_map/all_gather | solution.py:55
  37.2 25.9 %all-gather.5.cloned.1.call-start = ((), (), s32[]{:S(2)}) async-start(), calls=%async_computation.5 | async-start | bytes 1572864 | tf_op jit(solution)/shard_map/all_gather | solution.py:56
  61.2 1.9 copy-start.3
  61.5 3.6 %copy-start.8 = (f32[128]{0:T(128)S(1)}, f32[128]{0:T(128)}, u32[]{:S(2)}) copy-start(f32[128]{0:T(128)} %param.15) | copy-start | bytes 1540
  63.1 2.4 copy-start
  63.1 2.0 copy-start.1
  65.1 0.9 copy-start.6
  69.6 29.5 %all-to-all-start.2 = ((bf16[16,128,256]{2,1,0:T(8,128)(2,1)}), bf16[16,128,256]{2,1,0:T(8,128)(2,1)S(1)}, u32[]{:S(2)}, u32[]{:S(2)}) async-start(bf16[16,128,256]{2,1,0:T(8,128)(2,1)} %bitcast.3), calls=%async_computation.3 | async-start | bytes 2097152 | tf_op jit(solution)/shard_map/all_to_all | solution.py:93
  75.4 48.3 %all-reduce.3.cloned.1.call-start = ((), (), s32[]{:S(2)}) async-start(), calls=%async_computation.7 | async-start | bytes 1048576 | tf_op jit(solution)/shard_map/psum | solution.py:99
  104.6 32.1 %reduce-scatter.2.cloned.1.call-start = ((), (), s32[]{:S(2)}) async-start(), calls=%async_computation.6 | async-start | bytes 3145728 | tf_op jit(solution)/shard_map/reduce_scatter | solution.py:73
  106.7 18.3 %copy-start.5 = (f32[1024]{0:T(1024)S(1)}, f32[1024]{0:T(1024)}, u32[]{:S(2)}) copy-start(f32[1024]{0:T(1024)} %param.10) | copy-start | bytes 12292
Sparse Core Ops, SparseCore 0:
  38.9 10.2 all-gather.2
  50.7 10.1 all-gather.4
  104.8 18.9 all-reduce.2
  125.9 10.7 reduce-scatter.1
where the time goes:
time: 248 us; the launch traced here: 247 us
  blocking collectives  116 us (47%)
  waiting for transfers between devices  72.1 us (29%)
  matrix products  21.7 us (9%)
  between operations  14 us (6%)
  starting transfers between devices  9.95 us (4%)
  local copies, waits for them, and re-layouts  7.88 us (3%)
  other arithmetic  5.22 us (2%)
    psum x1, blocking collectives, local(): grand_total = lax.psum(narrow_sum, 'table')  101 us
    all_to_all x1, waiting for transfers between devices, local(): lax.all_to_all(slot_grads, 'table', split_axis=0, concat_axis=0, tiled=True)  23 us
    all_to_all x1, waiting for transfers between devices, local(): lax.all_to_all(pool_out, 'table', split_axis=0, concat_axis=0, tiled=True)  21.7 us
    psum x1, waiting for transfers between devices, local(): lax.psum(local_grad.astype(jnp.bfloat16), 'narrow').astype(jnp.float32)  17 us
    all_to_all x1, blocking collectives, local(): lax.all_to_all(bag_rows, 'table', split_axis=0, concat_axis=0, tiled=True)  15.5 us
    dot_general x4, matrix products, transposed_dot(): lax.dot_general(left, right, (((0,), (0,)), ((), ())), preferred_element_...  9.82 us
    reduce_scatter x1, waiting for transfers between devices, local(): lax.psum_scatter(jnp.concatenate([transposed_dot(pooled_feats, dhidden),...  8.95 us
    dot_general x1, matrix products, local(): pool_sums = jnp.dot(counts, table_rows, preferred_element_type=jnp.float32)  6.07 us
  transfers between devices with their start and end apart: 6, of which 4 were waited for; matrix products, arithmetic and copies ran while one was open for 4% of the time, Pallas kernels for 0%

commit v1 on v0

--- a/solution.py
+++ b/solution.py
@@ -78,7 +78,15 @@
         scatter_dimension=0,
         tiled=True,
     ).astype(jnp.float32)
-    grand_total = lax.psum(narrow_sum, "table")
+    degree = jax.lax.psum(1, axis_name="table")
+    grand_total, t_next = (narrow_sum, 0)
+    while 1 << t_next < degree:
+        seen = []
+        for i0 in tuple(range(degree)):
+            seen.append((i0, i0 ^ 1 << t_next))
+        earlier = jax.lax.ppermute(grand_total, axis_name="table", perm=seen)
+        grand_total = grand_total + earlier
+        t_next = t_next + 1
     batch_all = samples * tables * narrows
     grand_total = grand_total * (1.0 / math.sqrt(batch_all))
     rank_size = factor_down.shape[1]

time: 248 us -> 339 us (1.37)
  waiting for transfers between devices: 72.1 us -> 249 us
  blocking collectives: 116 us -> 15.5 us
  other arithmetic: 5.22 us -> 12.1 us
  starting transfers between devices: 9.95 us -> 15.3 us
    ppermute x0 -> x4, waiting for transfers between devices: none -> 193 us  [local(): earlier = jax.lax.ppermute(grand_total, axis_name='table', perm=seen)]
    psum x1 -> x0, blocking collectives: 101 us -> none  [local(): grand_total = lax.psum(narrow_sum, 'table')]
    all_to_all x1, waiting for transfers between devices: 23 us -> 5.97 us  [local(): lax.all_to_all(slot_grads, 'table', split_axis=0, concat_axis=0, tiled=True)]
    ppermute x0 -> x4, starting transfers between devices: none -> 5.51 us  [local(): earlier = jax.lax.ppermute(grand_total, axis_name='table', perm=seen)]
    add x0 -> x3, other arithmetic: none -> 3.44 us  [local(): grand_total = grand_total + earlier]
  transfers between devices with their start and end apart: 6 -> 10, of which waited for: 4 -> 8; matrix products, arithmetic and copies ran while one was open for 4% -> 7% of each run, Pallas kernels for 0% -> 0%
where the time goes in v1:
time: 339 us; the launch traced here: 338 us
  waiting for transfers between devices  249 us (73%)
  matrix products  23.7 us (7%)
  blocking collectives  15.5 us (5%)
  starting transfers between devices  15.3 us (5%)
  between operations  14 us (4%)
  other arithmetic  12.1 us (4%)
  local copies, waits for them, and re-layouts  8.82 us (3%)
    ppermute x4, waiting for transfers between devices, local(): earlier = jax.lax.ppermute(grand_total, axis_name='table', perm=seen)  193 us
    all_to_all x1, waiting for transfers between devices, local(): lax.all_to_all(pool_out, 'table', split_axis=0, concat_axis=0, tiled=True)  21.7 us
    psum x1, waiting for transfers between devices, local(): lax.psum(local_grad.astype(jnp.bfloat16), 'narrow').astype(jnp.float32)  17 us
    all_to_all x1, blocking collectives, local(): lax.all_to_all(bag_rows, 'table', split_axis=0, concat_axis=0, tiled=True)  15.5 us
    dot_general x4, matrix products, transposed_dot(): lax.dot_general(left, right, (((0,), (0,)), ((), ())), preferred_element_...  11.1 us
    reduce_scatter x1, waiting for transfers between devices, local(): lax.psum_scatter(jnp.concatenate([transposed_dot(pooled_feats, dhidden),...  9.97 us
  transfers between devices with their start and end apart: 10, of which 8 were waited for; matrix products, arithmetic and copies ran while one was open for 7% of the time, Pallas kernels for 0%

profile of v1, /device:TPU:0, one launch (start us, length us, event | category | flops | bytes accessed | tf_op | source)
XLA Modules:
  0.0 338.1 jit_solution(13713627515984569368)
XLA Ops:
  8.0 15.5 %all_to_all.19 = s32[16,1,512]{2,1,0:T(1,128)S(1)} all-to-all(s32[16,1,512]{2,1,0:T(1,128)S(1)} %all_to_all.12), channel_id=1, replica_groups=mesh['table'=16,'narrow'=2] {'table'}, dimensions={0} | all-to-all | bytes 65536 | tf_op jit(solution)/shard_map/all_to_all | solution.py:36
  23.5 1.1 reshape.40
  24.6 2.0 slice_reduce_fusion.3
  26.6 6.1 %fusion.15 = bf16[2048,256]{1,0:T(8,128)(2,1)} fusion(bf16[1024,256]{1,0:T(8,128)(2,1)S(1)} %copy-done.4, s32[2048]{0:T(1024)S(1)} %get-tuple-element.21, s32[2048]{0:T(1024)S(1)} %get-tuple-element.22, s32[2048]{0:T(1024)S(1)} %get-tuple-element.23, s32[2048]{0:T(1024)S(1)} %get-tuple-element.20), kind=kOutput, calls=%fused_computation.18 | convolution fusion | flops 1107820544 | bytes 1605632 | tf_op jit(solution)/shard_map/dot_general | solution.py:42
  32.7 3.8 %all-to-all-start.1 = ((bf16[16,128,256]{2,1,0:T(8,128)(2,1)}), bf16[16,128,256]{2,1,0:T(8,128)(2,1)S(1)}, u32[]{:S(2)}, u32[]{:S(2)}) async-start(bf16[16,128,256]{2,1,0:T(8,128)(2,1)} %bitcast.1), calls=%async_computation.1 | async-start | bytes 2097152 | tf_op jit(solution)/shard_map/all_to_all | solution.py:44
  38.0 21.7 %all-to-all-done.1 = bf16[16,128,256]{2,1,0:T(8,128)(2,1)S(1)} async-done(((bf16[16,128,256]{2,1,0:T(8,128)(2,1)}), bf16[16,128,256]{2,1,0:T(8,128)(2,1)S(1)}, u32[]{:S(2)}, u32[]{:S(2)}) %all-to-all-start.1) | async-done | bytes 1048608 | tf_op jit(solution)/shard_map/all_to_all | solution.py:44
  59.7 1.5 fusion.23
  61.5 1.5 convolution_convert_fusion.3
  63.1 1.9 fusion.29
  66.4 1.6 pad_maximum_fusion
  68.1 10.0 %reduce-scatter.2.cloned.1.call-done = bf16[1024,512]{0,1:T(8,128)(2,1)} async-done(((bf16[2048,512]{0,1:T(8,128)(2,1)}), bf16[1024,512]{0,1:T(8,128)(2,1)}) %reduce-scatter.2.cloned.1.call-update) | async-done | bytes 1048592 | tf_op jit(solution)/shard_map/reduce_scatter | solution.py:73
  78.0 1.5 convert_element_type.67
  79.6 1.8 collective-permute-start
  81.4 46.1 %collective-permute-done = f32[1024,512]{0,1:T(8,128)S(1)} collective-permute-done((f32[1024,512]{0,1:T(8,128)S(1)}, f32[1024,512]{0,1:T(8,128)S(1)}, u32[]{:S(2)}, u32[]{:S(2)}) %collective-permute-start) | collective-permute-done | bytes 2097184 | tf_op jit(solution)/shard_map/ppermute | solution.py:87
  127.9 1.8 collective-permute-start.1
  129.7 45.3 %collective-permute-done.1 = f32[1024,512]{0,1:T(8,128)S(1)} collective-permute-done((f32[1024,512]{0,1:T(8,128)S(1)}, f32[1024,512]{0,1:T(8,128)S(1)}, u32[]{:S(2)}, u32[]{:S(2)}) %collective-permute-start.1) | collective-permute-done | bytes 2097184 | tf_op jit(solution)/shard_map/ppermute | solution.py:87
  175.4 1.8 collective-permute-start.2
  177.3 1.3 fusion.19
  178.5 1.3 reshape.44
  179.8 3.3 fusion.18
  183.2 5.6 %all-to-all-start.2 = ((bf16[16,128,256]{2,1,0:T(8,128)(2,1)}), bf16[16,128,256]{2,1,0:T(8,128)(2,1)}, u32[]{:S(2)}, u32[]{:S(2)}) async-start(bf16[16,128,256]{2,1,0:T(8,128)(2,1)} %bitcast.3), calls=%async_computation.3 | async-start | bytes 2097152 | tf_op jit(solution)/shard_map/all_to_all | solution.py:101
  189.0 46.3 %collective-permute-done.2 = f32[1024,512]{0,1:T(8,128)} collective-permute-done((f32[1024,512]{0,1:T(8,128)S(1)}, f32[1024,512]{0,1:T(8,128)}, u32[]{:S(2)}, u32[]{:S(2)}) %collective-permute-start.2) | collective-permute-done | bytes 2097184 | tf_op jit(solution)/shard_map/ppermute | solution.py:87
  235.3 2.6 add.69
  238.0 6.0 %all-to-all-done.2 = bf16[16,128,256]{2,1,0:T(8,128)(2,1)} async-done(((bf16[16,128,256]{2,1,0:T(8,128)(2,1)}), bf16[16,128,256]{2,1,0:T(8,128)(2,1)}, u32[]{:S(2)}, u32[]{:S(2)}) %all-to-all-start.2) | async-done | bytes 1048608 | tf_op jit(solution)/shard_map/all_to_all | solution.py:101
  244.0 6.8 %fusion.20 = bf16[1024,256]{1,0:T(8,128)(2,1)} fusion(bf16[2048,256]{1,0:T(8,128)(2,1)} %bitcast.4, s32[2048]{0:T(1024)S(1)} %get-tuple-element.21, s32[2048]{0:T(1024)S(1)} %get-tuple-element.22, s32[2048]{0:T(1024)S(1)} %get-tuple-element.23, s32[2048]{0:T(1024)S(1)} %get-tuple-element.20), kind=kOutput, calls=%fused_computation.32 | convolution fusion | flops 1107558400 | bytes 1605632 | tf_op jit(solution)/shard_map/dot_general | solution.py:15
  250.8 17.0 %all-reduce.2.cloned.1.call-done = bf16[1024,256]{1,0:T(8,128)(2,1)} async-done(((bf16[1024,256]{1,0:T(8,128)(2,1)}), bf16[1024,256]{1,0:T(8,128)(2,1)}) %all-reduce.2.cloned.1.call-update) | async-done | bytes 524304 | tf_op jit(solution)/shard_map/psum | solution.py:107
  267.8 1.3 fusion.24
  269.8 2.1 fusion.26
  271.9 54.9 %collective-permute-done.3 = f32[1024,512]{0,1:T(8,128)} collective-permute-done((f32[1024,512]{0,1:T(8,128)S(1)}, f32[1024,512]{0,1:T(8,128)}, u32[]{:S(2)}, u32[]{:S(2)}) %collective-permute-start.3) | collective-permute-done | bytes 2097184 | tf_op jit(solution)/shard_map/ppermute | solution.py:87
  326.8 2.0 add_multiply_fusion
  328.9 1.3 copy.19
  330.2 1.3 copy.18
  (48 shorter events, 6.0 us)
Async XLA Ops:
  24.6 2.0 copy-start.4
  32.7 5.3 %copy-start.7 = (bf16[2048]{0:T(1024)(128)(2,1)S(1)}, bf16[2048]{0:T(1024)(128)(2,1)}, u32[]{:S(2)}) copy-start(bf16[2048]{0:T(1024)(128)(2,1)} %param.14) | copy-start | bytes 12292
  32.7 27.1 %copy-start.10 = (s32[16,128]{1,0:T(8,128)S(1)}, s32[16,128]{1,0:T(8,128)}, u32[]{:S(2)}) copy-start(s32[16,128]{1,0:T(8,128)} %param.17) | copy-start | bytes 24580
  32.7 27.1 %all-to-all-start.1 = ((bf16[16,128,256]{2,1,0:T(8,128)(2,1)}), bf16[16,128,256]{2,1,0:T(8,128)(2,1)S(1)}, u32[]{:S(2)}, u32[]{:S(2)}) async-start(bf16[16,128,256]{2,1,0:T(8,128)(2,1)} %bitcast.1), calls=%async_computation.1 | async-start | bytes 2097152 | tf_op jit(solution)/shard_map/all_to_all | solution.py:44
  36.5 25.0 %all-gather.3.cloned.1.call-start = ((), (), s32[]{:S(2)}) async-start(), calls=%async_computation.4 | async-start | bytes 1572864 | tf_op jit(solution)/shard_map/all_gather | solution.py:55
  37.2 25.8 %all-gather.5.cloned.1.call-start = ((), (), s32[]{:S(2)}) async-start(), calls=%async_computation.5 | async-start | bytes 1572864 | tf_op jit(solution)/shard_map/all_gather | solution.py:56
  38.0 40.1 %reduce-scatter.2.cloned.1.call-start = ((), (), s32[]{:S(2)}) async-start(), calls=%async_computation.6 | async-start | bytes 3145728 | tf_op jit(solution)/shard_map/reduce_scatter | solution.py:73
  61.2 1.9 copy-start.6
  61.5 3.6 %copy-start.11 = (f32[128]{0:T(128)S(1)}, f32[128]{0:T(128)}, u32[]{:S(2)}) copy-start(f32[128]{0:T(128)} %param.15) | copy-start | bytes 1540
  63.1 2.5 copy-start.3
  65.0 1.4 copy-start.9
  78.0 49.4 %copy-start.1 = (bf16[1024,512]{0,1:T(8,128)(2,1)S(1)}, bf16[1024,512]{0,1:T(8,128)(2,1)}, u32[]{:S(2)}) copy-start(bf16[1024,512]{0,1:T(8,128)(2,1)} %reduce-scatter.2.cloned.1.call-done) | copy-start | bytes 3145732
  79.6 47.9 %collective-permute-start = (f32[1024,512]{0,1:T(8,128)S(1)}, f32[1024,512]{0,1:T(8,128)S(1)}, u32[]{:S(2)}, u32[]{:S(2)}) collective-permute-start(f32[1024,512]{0,1:T(8,128)S(1)} %convert_element_type.67), channel_id=1, source_target_pairs={{0,2},{2,0},{4,6},{6,4},{8,10},{10,8},{12,14},{14,12},{16,18},{18,... | collective-permute-start | bytes 6291464 | tf_op jit(solution)/shard_map/ppermute | solution.py:87
  127.9 49.3 %copy-start.2 = (bf16[2048,256]{1,0:T(8,128)(2,1)S(1)}, bf16[2048,256]{1,0:T(8,128)(2,1)}, u32[]{:S(2)}) copy-start(bf16[2048,256]{1,0:T(8,128)(2,1)} %all-gather.3.cloned.1.call-done) | copy-start | bytes 3145732
  127.9 47.1 %collective-permute-start.1 = (f32[1024,512]{0,1:T(8,128)S(1)}, f32[1024,512]{0,1:T(8,128)S(1)}, u32[]{:S(2)}, u32[]{:S(2)}) collective-permute-start(f32[1024,512]{0,1:T(8,128)S(1)} %convert_add_fusion), channel_id=1, source_target_pairs={{0,4},{2,6},{4,0},{6,2},{8,12},{10,14},{12,8},{14,10},{16,20},{18,... | collective-permute-start | bytes 6291464 | tf_op jit(solution)/shard_map/ppermute | solution.py:87
  175.4 7.8 %copy-start = (f32[1024,512]{0,1:T(8,128)}, f32[1024,512]{0,1:T(8,128)S(1)}, u32[]{:S(2)}) copy-start(f32[1024,512]{0,1:T(8,128)S(1)} %add.68) | copy-start | bytes 6291460
  175.4 59.9 %collective-permute-start.2 = (f32[1024,512]{0,1:T(8,128)S(1)}, f32[1024,512]{0,1:T(8,128)}, u32[]{:S(2)}, u32[]{:S(2)}) collective-permute-start(f32[1024,512]{0,1:T(8,128)S(1)} %add.68), channel_id=1, source_target_pairs={{0,8},{2,10},{4,12},{6,14},{8,0},{10,2},{12,4},{14,6},{16,24},{18,... | collective-permute-start | bytes 6291464 | tf_op jit(solution)/shard_map/ppermute | solution.py:87
  183.2 60.8 %all-to-all-start.2 = ((bf16[16,128,256]{2,1,0:T(8,128)(2,1)}), bf16[16,128,256]{2,1,0:T(8,128)(2,1)}, u32[]{:S(2)}, u32[]{:S(2)}) async-start(bf16[16,128,256]{2,1,0:T(8,128)(2,1)} %bitcast.3), calls=%async_computation.3 | async-start | bytes 2097152 | tf_op jit(solution)/shard_map/all_to_all | solution.py:101
  188.8 79.0 %all-reduce.2.cloned.1.call-start = ((), (), s32[]{:S(2)}) async-start(), calls=%async_computation.7 | async-start | bytes 1048576 | tf_op jit(solution)/shard_map/psum | solution.py:107
  238.0 88.8 %collective-permute-start.3 = (f32[1024,512]{0,1:T(8,128)S(1)}, f32[1024,512]{0,1:T(8,128)}, u32[]{:S(2)}, u32[]{:S(2)}) collective-permute-start(f32[1024,512]{0,1:T(8,128)S(1)} %add.69), channel_id=1, source_target_pairs={{0,16},{2,18},{4,20},{6,22},{8,24},{10,26},{12,28},{14,30},{16,0},... | collective-permute-start | bytes 6291464 | tf_op jit(solution)/shard_map/ppermute | solution.py:87
  244.0 25.1 %copy-start.8 = (f32[1024]{0:T(1024)S(1)}, f32[1024]{0:T(1024)}, u32[]{:S(2)}) copy-start(f32[1024]{0:T(1024)} %param.10) | copy-start | bytes 12292
  244.0 25.7 %copy-start.5 = (bf16[1024,256]{1,0:T(8,128)(2,1)S(1)}, bf16[1024,256]{1,0:T(8,128)(2,1)}, u32[]{:S(2)}) copy-start(bf16[1024,256]{1,0:T(8,128)(2,1)} %param.9) | copy-start | bytes 1572868
Sparse Core Ops, SparseCore 0:
  38.9 10.2 all-gather.2
  50.7 10.1 all-gather.4
  68.2 9.8 reduce-scatter.1
  250.9 16.8 all-reduce.1
